TPU v7x, 32 devices: a whole 2x2x4 slice. The times are simulated.
32 devices in a mesh: dp: 8 (over z, y), tensor: 4 (over x, core).
Axes of the slice: x: 2, y: 2, z: 4, core: 2. Of those that a mesh axis runs over, the one named last changes fastest.
Arguments:
- tokens: bfloat16 [4096, 2048], P(('dp', 'tensor')), may hold values from -6 to 6
- lengths: int32 [8, 4], P('dp'), may hold values from 0 to 512, as said below
- w_query: bfloat16 [2048, 2048], P(None, 'tensor'), may hold values from -0.125 to 0.125
- w_key: bfloat16 [2048, 2048], P(None, 'tensor'), may hold values from -0.125 to 0.125
- w_value: bfloat16 [2048, 2048], P(None, 'tensor'), may hold values from -0.125 to 0.125
- w_out: bfloat16 [2048, 2048], P('tensor'), may hold values from -0.125 to 0.125
- w_gate: bfloat16 [2048, 8192], P(None, 'tensor'), may hold values from -0.125 to 0.125
- w_up: bfloat16 [2048, 8192], P(None, 'tensor'), may hold values from -0.125 to 0.125
- w_down: bfloat16 [8192, 2048], P('tensor'), may hold values from -0.0625 to 0.0625
- gain_query: float32 [2048], P('tensor'), may hold values from 0.1 to 1.9
- gain_key: float32 [2048], P('tensor'), may hold values from 0.1 to 1.9
- gain_attn: float32 [2048], replicated, may hold values from 0.1 to 1.9
- gain_mlp: float32 [2048], replicated, may hold values from 0.1 to 1.9
- cotangent: bfloat16 [4096, 2048], P(('dp', 'tensor')), may hold values from -6 to 6
Outputs:
- output: bfloat16 [4096, 2048], P(('dp', 'tensor'))
- grad_tokens: bfloat16 [4096, 2048], P(('dp', 'tensor'))
- grad_w_query: float32 [2048, 2048], P('dp', 'tensor')
- grad_w_key: float32 [2048, 2048], P('dp', 'tensor')
- grad_w_value: float32 [2048, 2048], P('dp', 'tensor')
- grad_w_out: float32 [2048, 2048], P('tensor', 'dp')
- grad_w_gate: float32 [2048, 8192], P('dp', 'tensor')
- grad_w_up: float32 [2048, 8192], P('dp', 'tensor')
- grad_w_down: float32 [8192, 2048], P('tensor', 'dp')
- grad_gain_query: float32 [2048], P('tensor')
- grad_gain_key: float32 [2048], P('tensor')
- grad_gain_attn: float32 [2048], replicated
- grad_gain_mlp: float32 [2048], replicated
Inputs may be any that keep to these rules, and one draw needn't show every extreme that they name: Each row lists the lengths of its sequences in order, then zeros; every nonzero length is 128 or more and they sum to 512; row 0 holds one sequence of 512 tokens.
All inputs are finite; a program needn't handle non-finite values.
Results may differ from a plain program's by a relative error of at most 0.023.
Values may be sent and summed in bfloat16 or wider, within the bound.
A program may use at most 256 MiB of HBM per device.

v0:
```python
import math
import jax
import jax.numpy as jnp
from jax import lax
from jax.sharding import PartitionSpec as P

HD = 128
ROW_LEN = 512
EPS = 1e-06
THETA = 500000.0


def rotate(values, offsets, rot_sign):
    half_width = values.shape[-1] // 2
    frequency = jnp.exp(
        jnp.arange(half_width, dtype=jnp.float32) * (-2.0 * math.log(THETA) / values.shape[-1])
    )
    angles = offsets.astype(jnp.float32)[..., None, None] * frequency
    cosines = jnp.cos(angles)
    sine_part = rot_sign * jnp.sin(angles)
    first_half = values[..., :half_width]
    second_half = values[..., half_width:]
    return jnp.concatenate(
        [
            first_half * cosines - second_half * sine_part,
            second_half * cosines + first_half * sine_part,
        ],
        axis=-1,
    )


def row_layout(lengths_row):
    slots = jnp.arange(lengths_row.shape[0], dtype=jnp.int32)
    seq_ends = jnp.sum(jnp.where(slots[None, :] <= slots[:, None], lengths_row[None, :], 0), axis=1)
    position = jnp.arange(ROW_LEN, dtype=jnp.int32)
    passed = (position[:, None] >= seq_ends[None, :]).astype(jnp.int32)
    segment = jnp.sum(passed, axis=1)
    seq_start = jnp.sum(passed * lengths_row[None, :], axis=1)
    return (segment, position - seq_start)


def allowed_mask(segment):
    position = jnp.arange(segment.shape[0], dtype=jnp.int32)
    return (segment[:, None] == segment[None, :]) & (position[None, :] <= position[:, None])


def times_t(left_mat, right_mat):
    return lax.dot_general(
        left_mat, right_mat, (((1,), (1,)), ((), ())), preferred_element_type=jnp.float32
    )


def t_times(left_mat, right_mat):
    return lax.dot_general(
        left_mat, right_mat, (((0,), (0,)), ((), ())), preferred_element_type=jnp.float32
    )


def masked_scores(queries_low, keys_low, segment):
    scale_factor = 1.0 / math.sqrt(queries_low.shape[-1])
    scores = (
        jnp.einsum("qhd,khd->hqk", queries_low, keys_low, preferred_element_type=jnp.float32)
        * scale_factor
    )
    return jnp.where(allowed_mask(segment)[None], scores, -1e30)


def attend(block_item):
    queries_low, keys_low, values_low, segment = block_item
    scores = masked_scores(queries_low, keys_low, segment)
    row_max = jnp.max(scores, axis=-1, keepdims=True)
    shifted = jnp.exp(scores - row_max)
    row_total = jnp.sum(shifted, axis=-1, keepdims=True)
    attn_weights = (shifted / row_total).astype(jnp.bfloat16)
    mixed = jnp.einsum("hqk,khd->qhd", attn_weights, values_low, preferred_element_type=jnp.float32)
    return (mixed.astype(jnp.bfloat16), (row_max + jnp.log(row_total))[..., 0])


def attend_back(block_item):
    queries_low, keys_low, values_low, segment, log_total, grad_mixed = block_item
    scale_factor = 1.0 / math.sqrt(queries_low.shape[-1])
    scores = masked_scores(queries_low, keys_low, segment)
    attn_weights = jnp.exp(scores - log_total[..., None])
    grad_weights = jnp.einsum(
        "qhd,khd->hqk", grad_mixed, values_low, preferred_element_type=jnp.float32
    )
    row_dots = jnp.sum(attn_weights * grad_weights, axis=-1, keepdims=True)
    grad_scores = (attn_weights * (grad_weights - row_dots)).astype(jnp.bfloat16)
    grad_queries = scale_factor * jnp.einsum(
        "hqk,khd->qhd", grad_scores, keys_low, preferred_element_type=jnp.float32
    )
    grad_keys = scale_factor * jnp.einsum(
        "hqk,qhd->khd", grad_scores, queries_low, preferred_element_type=jnp.float32
    )
    grad_values = jnp.einsum(
        "hqk,qhd->khd",
        attn_weights.astype(jnp.bfloat16),
        grad_mixed,
        preferred_element_type=jnp.float32,
    )
    return (grad_queries, grad_keys, grad_values.astype(jnp.bfloat16))


def post_norm_back(grad_in, unit_rows, inv_scale, gain_vec):
    scaled = grad_in * gain_vec
    mean_dots = jnp.mean(scaled * unit_rows, axis=-1, keepdims=True)
    return (inv_scale * (scaled - unit_rows * mean_dots), jnp.sum(grad_in * unit_rows, axis=0))


OUTER = 4


def swap(value, shift):
    size = lax.axis_size("dp")
    return lax.ppermute(value, "dp", [(d, d ^ shift) for d in range(size)])


def pick(parts, index):
    return lax.dynamic_index_in_dim(parts, index, 0, keepdims=False)


def sum_inner(parts):
    inner = parts.shape[0]
    mine = lax.axis_index("dp") % inner
    total = pick(parts, mine)
    for k in range(1, inner):
        sent = pick(parts, mine ^ k).astype(jnp.bfloat16)
        total = total + swap(sent, k).astype(jnp.float32)
    return total


def trade_outer(parts, inner):
    mine = lax.axis_index("dp") // inner
    got = [(mine, pick(parts, mine))]
    for k in range(1, OUTER):
        got.append((mine ^ k, swap(pick(parts, mine ^ k), k * inner)))
    return got


def split_rows(grad, inner):
    cols = grad.shape[1]
    return grad.reshape(OUTER, inner, -1, cols).transpose(1, 0, 2, 3)


def split_cols(grad, inner):
    rows = grad.shape[0]
    return grad.reshape(rows, OUTER, inner, -1).transpose(2, 1, 0, 3)


def scatter_sum(parts, inner):
    half = sum_inner(parts).astype(jnp.bfloat16)
    got = trade_outer(half, inner)
    return sum((g.astype(jnp.float32) for _, g in got))


def scatter_join(parts, inner, axis):
    half = sum_inner(parts).astype(jnp.bfloat16)
    got = trade_outer(half, inner)
    stack = jnp.zeros((OUTER, *got[0][1].shape), jnp.bfloat16)
    for place, block in got:
        stack = lax.dynamic_update_index_in_dim(stack, block, place, 0)
    joined = jnp.concatenate([stack[z] for z in range(OUTER)], axis=axis)
    return joined.astype(jnp.float32)


def body(
    tokens,
    lengths,
    w_query,
    w_key,
    w_value,
    w_out,
    w_gate,
    w_up,
    w_down,
    gain_query,
    gain_key,
    gain_attn,
    gain_mlp,
    cotangent,
):
    rows_dev = lengths.shape[0]
    model_width = w_query.shape[0]
    local_width = w_query.shape[1]
    head_count = local_width // HD
    gathered = lax.all_gather(tokens, "tensor", axis=0, tiled=True)
    row_count = gathered.shape[0]
    segment, offsets = jax.vmap(row_layout)(lengths)
    queries = jnp.dot(gathered, w_query, preferred_element_type=jnp.float32)
    keys_raw = jnp.dot(gathered, w_key, preferred_element_type=jnp.float32)
    values_low = jnp.dot(gathered, w_value, preferred_element_type=jnp.float32).astype(jnp.bfloat16)
    q_total, k_total = lax.psum(
        (jnp.sum(queries * queries, axis=1), jnp.sum(keys_raw * keys_raw, axis=1)), "tensor"
    )
    q_inv = lax.rsqrt(q_total / model_width + EPS)[:, None]
    k_inv = lax.rsqrt(k_total / model_width + EPS)[:, None]
    q_unit = queries * q_inv
    k_unit = keys_raw * k_inv

    def to_heads(values):
        return values.reshape(rows_dev, ROW_LEN, head_count, HD)

    queries_low = rotate(to_heads(q_unit * gain_query), offsets, 1.0).astype(jnp.bfloat16)
    keys_low = rotate(to_heads(k_unit * gain_key), offsets, 1.0).astype(jnp.bfloat16)
    values_heads = to_heads(values_low)
    mixed_heads, log_total = jax.vmap(lambda *a: attend(a))(
        queries_low, keys_low, values_heads, segment
    )
    mixed_low = mixed_heads.reshape(row_count, local_width)
    attn_out = lax.psum_scatter(
        jnp.dot(mixed_low, w_out, preferred_element_type=jnp.float32).astype(jnp.bfloat16),
        "tensor",
        scatter_dimension=0,
        tiled=True,
    ).astype(jnp.float32)
    a_inv = lax.rsqrt(jnp.mean(attn_out * attn_out, axis=1, keepdims=True) + EPS)
    a_unit = attn_out * a_inv
    hidden = tokens.astype(jnp.float32) + a_unit * gain_attn
    hidden_low = hidden.astype(jnp.bfloat16)
    hidden_all = lax.all_gather(hidden_low, "tensor", axis=0, tiled=True)
    inner_count = lax.axis_size("dp") // OUTER
    outer_index = lax.axis_index("dp") // inner_count

    def gather_group(shard):
        groups = [[z * inner_count + i for z in range(OUTER)] for i in range(inner_count)]
        part = lax.all_gather(shard, "dp", axis=0, tiled=True, axis_index_groups=groups)
        return lax.all_gather(part, "tensor", axis=0, tiled=True)

    hidden_group = gather_group(hidden_low)
    gate_acts = jnp.dot(hidden_all, w_gate, preferred_element_type=jnp.float32)
    up_acts = jnp.dot(hidden_all, w_up, preferred_element_type=jnp.float32)
    gate_sigmoid = jax.nn.sigmoid(gate_acts)
    inner_low = (gate_acts * gate_sigmoid * up_acts).astype(jnp.bfloat16)
    mlp_out = lax.psum_scatter(
        jnp.dot(inner_low, w_down, preferred_element_type=jnp.float32).astype(jnp.bfloat16),
        "tensor",
        scatter_dimension=0,
        tiled=True,
    ).astype(jnp.float32)
    f_inv = lax.rsqrt(jnp.mean(mlp_out * mlp_out, axis=1, keepdims=True) + EPS)
    f_unit = mlp_out * f_inv
    output = (hidden + f_unit * gain_mlp).astype(jnp.bfloat16)
    grad_output = cotangent.astype(jnp.float32)
    grad_mlp, grad_gain_mlp_part = post_norm_back(grad_output, f_unit, f_inv, gain_mlp)
    grad_mlp_low = grad_mlp.astype(jnp.bfloat16)
    mlp_grad_all = lax.all_gather(grad_mlp_low, "tensor", axis=0, tiled=True)
    mlp_grad_group = gather_group(grad_mlp_low)
    grad_inner = times_t(mlp_grad_all, w_down)
    grad_gate_low = (
        grad_inner * up_acts * gate_sigmoid * (1.0 + gate_acts * (1.0 - gate_sigmoid))
    ).astype(jnp.bfloat16)
    grad_up_low = (grad_inner * gate_acts * gate_sigmoid).astype(jnp.bfloat16)
    part_width = w_gate.shape[1] // OUTER
    gate_part = lax.dynamic_slice_in_dim(w_gate, outer_index * part_width, part_width, 1)
    up_part = lax.dynamic_slice_in_dim(w_up, outer_index * part_width, part_width, 1)
    down_part = lax.dynamic_slice_in_dim(w_down, outer_index * part_width, part_width, 0)
    gate_g = jnp.dot(hidden_group, gate_part, preferred_element_type=jnp.float32)
    up_g = jnp.dot(hidden_group, up_part, preferred_element_type=jnp.float32)
    sig_g = jax.nn.sigmoid(gate_g)
    inner_g = (gate_g * sig_g * up_g).astype(jnp.bfloat16)
    grad_inner_g = times_t(mlp_grad_group, down_part)
    grad_gate_g = (grad_inner_g * up_g * sig_g * (1.0 + gate_g * (1.0 - sig_g))).astype(
        jnp.bfloat16
    )
    grad_up_g = (grad_inner_g * gate_g * sig_g).astype(jnp.bfloat16)
    sum_down = scatter_join(
        split_cols(t_times(inner_g, mlp_grad_group), inner_count), inner_count, 0
    )
    sum_gate = scatter_join(
        split_rows(t_times(hidden_group, grad_gate_g), inner_count), inner_count, 1
    )
    sum_up = scatter_join(split_rows(t_times(hidden_group, grad_up_g), inner_count), inner_count, 1)
    grad_hidden = grad_output + lax.psum_scatter(
        (times_t(grad_gate_low, w_gate) + times_t(grad_up_low, w_up)).astype(jnp.bfloat16),
        "tensor",
        scatter_dimension=0,
        tiled=True,
    ).astype(jnp.float32)
    grad_attn, grad_gain_attn_part = post_norm_back(grad_hidden, a_unit, a_inv, gain_attn)
    attn_grad_all = lax.all_gather(grad_attn.astype(jnp.bfloat16), "tensor", axis=0, tiled=True)
    grad_w_out = t_times(mixed_low, attn_grad_all)
    grad_mixed = times_t(attn_grad_all, w_out).astype(jnp.bfloat16)
    grad_q_rot, grad_k_rot, grad_values_low = jax.vmap(lambda *a: attend_back(a))(
        queries_low, keys_low, values_heads, segment, log_total, to_heads(grad_mixed)
    )
    grad_q_norm = rotate(grad_q_rot, offsets, -1.0).reshape(row_count, local_width)
    grad_k_norm = rotate(grad_k_rot, offsets, -1.0).reshape(row_count, local_width)
    grad_gain_query_part = jnp.sum(grad_q_norm * q_unit, axis=0)
    grad_gain_key_part = jnp.sum(grad_k_norm * k_unit, axis=0)
    q_scaled = grad_q_norm * gain_query
    k_scaled = grad_k_norm * gain_key
    q_dots, k_dots = lax.psum(
        (jnp.sum(q_scaled * q_unit, axis=1), jnp.sum(k_scaled * k_unit, axis=1)), "tensor"
    )
    grad_queries_low = (q_inv * (q_scaled - q_unit * (q_dots / model_width)[:, None])).astype(
        jnp.bfloat16
    )
    grad_keys_low = (k_inv * (k_scaled - k_unit * (k_dots / model_width)[:, None])).astype(
        jnp.bfloat16
    )
    grad_values_flat = grad_values_low.reshape(row_count, local_width)
    grad_w_query = t_times(gathered, grad_queries_low)
    grad_w_key = t_times(gathered, grad_keys_low)
    grad_w_value = t_times(gathered, grad_values_flat)
    grad_tokens = (
        grad_hidden
        + lax.psum_scatter(
            (
                times_t(grad_queries_low, w_query)
                + times_t(grad_keys_low, w_key)
                + times_t(grad_values_flat, w_value)
            ).astype(jnp.bfloat16),
            "tensor",
            scatter_dimension=0,
            tiled=True,
        ).astype(jnp.float32)
    ).astype(jnp.bfloat16)
    tensor_start = lax.axis_index("tensor") * local_width
    zero_row = jnp.zeros((model_width,), jnp.float32)
    q_full = lax.dynamic_update_slice(zero_row, grad_gain_query_part, (tensor_start,))
    k_full = lax.dynamic_update_slice(zero_row, grad_gain_key_part, (tensor_start,))
    gain_stack = jnp.stack([q_full, k_full, grad_gain_attn_part, grad_gain_mlp_part])
    gain_total = lax.psum(gain_stack, ("dp", "tensor"))
    grad_gain_query = lax.dynamic_slice(gain_total[0], (tensor_start,), (local_width,))
    grad_gain_key = lax.dynamic_slice(gain_total[1], (tensor_start,), (local_width,))
    summed = (
        scatter_sum(split_rows(grad_w_query, inner_count), inner_count),
        scatter_sum(split_rows(grad_w_key, inner_count), inner_count),
        scatter_sum(split_rows(grad_w_value, inner_count), inner_count),
        scatter_sum(split_cols(grad_w_out, inner_count), inner_count),
        sum_gate,
        sum_up,
        sum_down,
    )
    return (
        output,
        grad_tokens,
        summed[0],
        summed[1],
        summed[2],
        summed[3],
        summed[4],
        summed[5],
        summed[6],
        grad_gain_query,
        grad_gain_key,
        gain_total[2],
        gain_total[3],
    )


def solution(mesh):
    placed = (
        P(("dp", "tensor"), None),
        P("dp", None),
        P(None, "tensor"),
        P(None, "tensor"),
        P(None, "tensor"),
        P("tensor", None),
        P(None, "tensor"),
        P(None, "tensor"),
        P("tensor", None),
        P("tensor"),
        P("tensor"),
        P(),
        P(),
        P(("dp", "tensor"), None),
    )
    return jax.shard_map(
        body,
        mesh=mesh,
        in_specs=placed,
        out_specs=(
            P(("dp", "tensor"), None),
            P(("dp", "tensor"), None),
            P("dp", "tensor"),
            P("dp", "tensor"),
            P("dp", "tensor"),
            P("tensor", "dp"),
            P("dp", "tensor"),
            P("dp", "tensor"),
            P("tensor", "dp"),
            P("tensor"),
            P("tensor"),
            P(),
            P(),
        ),
        check_vma=False,
    )
```

profile of v0, /device:TPU:9, one launch (start us, length us, event | category | flops | bytes accessed | tf_op | source)
XLA Modules:
  0.0 888.0 jit_solution(406805340475882868)
XLA Ops:
  12.2 21.6 %all-gather.9.cloned.1.call-done = bf16[512,2048]{1,0:T(8,128)(2,1)} async-done(((bf16[128,2048]{1,0:T(8,128)(2,1)}), bf16[512,2048]{1,0:T(8,128)(2,1)}) %all-gather.9.cloned.1.call-update) | async-done | bytes 2097168 | tf_op jit(solution)/shard_map/all_gather | solution.py:186
  70.3 32.8 %reduce-scatter.5.cloned.1.call-done = bf16[128,2048]{1,0:T(8,128)(2,1)} async-done(((bf16[512,2048]{1,0:T(8,128)(2,1)}), bf16[128,2048]{1,0:T(8,128)(2,1)}) %reduce-scatter.5.cloned.1.call-update) | async-done | bytes 524304 | tf_op jit(solution)/shard_map/reduce_scatter | solution.py:210
  106.8 22.8 %all-gather.11.cloned.1.call-done = bf16[512,2048]{1,0:T(8,128)(2,1)} async-done(((bf16[128,2048]{1,0:T(8,128)(2,1)}), bf16[512,2048]{1,0:T(8,128)(2,1)}) %all-gather.11.cloned.1.call-update) | async-done | bytes 2097168 | tf_op jit(solution)/shard_map/all_gather | solution.py:220
  129.6 8.6 fusion.92
  138.2 8.4 fusion.93
  148.6 9.5 %convolution_convert_fusion = bf16[512,2048]{1,0:T(8,128)(2,1)} fusion(bf16[2048,2048]{1,0:T(8,128)(2,1)} %param.22, f32[512,2048]{1,0:T(8,128)S(1)} %fusion.93, f32[512,2048]{1,0:T(8,128)S(1)} %fusion.92), kind=kOutput, calls=%fused_computation.21 | convolution fusion | flops 4302307328 | bytes 18874368 | tf_op jit(solution)/shard_map/dot_general | solution.py:235
  158.2 31.1 %reduce-scatter.7.cloned.1.call-done = bf16[128,2048]{1,0:T(8,128)(2,1)} async-done(((bf16[512,2048]{1,0:T(8,128)(2,1)}), bf16[128,2048]{1,0:T(8,128)(2,1)}) %reduce-scatter.7.cloned.1.call-update) | async-done | bytes 524304 | tf_op jit(solution)/shard_map/reduce_scatter | solution.py:234
  194.3 23.1 %all-gather.13.cloned.1.call-done = bf16[512,2048]{1,0:T(8,128)(2,1)} async-done(((bf16[128,2048]{1,0:T(8,128)(2,1)}), bf16[512,2048]{1,0:T(8,128)(2,1)}) %all-gather.13.cloned.1.call-update) | async-done | bytes 2097168 | tf_op jit(solution)/shard_map/all_gather | solution.py:246
  217.4 7.6 fusion.94
  225.0 13.6 %fusion.25 = f32[512,2048]{1,0:T(8,128)} fusion(bf16[2048,2048]{1,0:T(8,128)(2,1)} %param.20, f32[512,2048]{1,0:T(8,128)} %copy-done.53, f32[512,2048]{1,0:T(8,128)S(1)} %fusion.94, f32[512,2048]{1,0:T(8,128)} %copy-done.54), kind=kOutput, calls=%fused_computation.56 | convolution fusion | flops 4305453056 | bytes 25165824 | tf_op jit(solution)/shard_map/dot_general | solution.py:48
  238.6 11.8 %add_convert_fusion.1 = bf16[512,2048]{1,0:T(8,128)(2,1)} fusion(f32[512,2048]{1,0:T(8,128)} %fusion.25, bf16[2048,2048]{1,0:T(8,128)(2,1)} %param.21, f32[512,2048]{1,0:T(8,128)S(1)} %fusion.94, f32[512,2048]{1,0:T(8,128)} %copy-done.53), kind=kOutput, calls=%fused_computation.8 | convolution fusion | flops 4303355904 | bytes 23068672 | tf_op jit(solution)/shard_map/dot_general | solution.py:48
  251.3 30.4 %reduce-scatter.9.cloned.1.call-done = bf16[128,2048]{1,0:T(8,128)(2,1)} async-done(((bf16[512,2048]{1,0:T(8,128)(2,1)}), bf16[128,2048]{1,0:T(8,128)(2,1)}) %reduce-scatter.9.cloned.1.call-update) | async-done | bytes 524304 | tf_op jit(solution)/shard_map/reduce_scatter | solution.py:273
  286.9 41.1 %all-gather.17.cloned.1.call-done = bf16[512,2048]{1,0:T(8,128)(2,1)} async-done(((bf16[128,2048]{1,0:T(8,128)(2,1)}), bf16[512,2048]{1,0:T(8,128)(2,1)}) %all-gather.17.cloned.1.call-update) | async-done | bytes 2097168 | tf_op jit(solution)/shard_map/all_gather | solution.py:226
  328.2 25.5 %all-gather.15.cloned.1.call-done = bf16[512,2048]{1,0:T(8,128)(2,1)} async-done(((bf16[128,2048]{1,0:T(8,128)(2,1)}), bf16[512,2048]{1,0:T(8,128)(2,1)}) %all-gather.15.cloned.1.call-update) | async-done | bytes 2097168 | tf_op jit(solution)/shard_map/all_gather | solution.py:280
  399.8 60.7 %all-gather.19.cloned.1.call-done = bf16[2048,2048]{1,0:T(8,128)(2,1)} async-done(((bf16[512,2048]{1,0:T(8,128)(2,1)}), bf16[2048,2048]{1,0:T(8,128)(2,1)}) %all-gather.19.cloned.1.call-update) | async-done | bytes 8388624 | tf_op jit(solution)/shard_map/all_gather | solution.py:227
  460.5 10.6 %fusion.14 = f32[2048,512]{1,0:T(8,128)} fusion(bf16[2048,2048]{1,0:T(8,128)(2,1)} %all-gather.19.cloned.1.call-done, bf16[2048,2048]{1,0:T(8,128)(2,1)} %param.20, s32[]{:T(128)S(6)} %select_n.141), kind=kOutput, calls=%fused_computation.44 | convolution fusion | flops 4294967296 | bytes 14680068 | tf_op jit(solution)/shard_map/dot_general | solution.py:257
  471.2 8.7 fusion.18
  505.5 6.8 reshape.573
  527.1 6.8 reshape.574
  554.8 71.2 %psum.39 = f32[4,2048]{1,0:T(4,128)S(1)} all-reduce(f32[4,2048]{1,0:T(4,128)S(1)} %pad_maximum_fusion.8), channel_id=1, replica_groups=mesh['dp'=8,'tensor'=4] {'dp','tensor'}, use_global_device_ids=true, to_apply=%region_26.27 | all-reduce | flops 8192 | bytes 65536 | tf_op jit(solution)/shard_map/psum | solution.py:323
  668.2 14.5 %collective-permute-done.2 = bf16[256,512]{1,0:T(8,128)(2,1)S(1)} collective-permute-done((bf16[256,512]{1,0:T(8,128)(2,1)S(1)}, bf16[256,512]{1,0:T(8,128)(2,1)S(1)}, u32[]{:S(2)}, u32[]{:S(2)}) %collective-permute-start.2) | collective-permute-done | bytes 262176 | tf_op jit(solution)/shard_map/ppermute | solution.py:115
  688.4 13.6 %collective-permute-done.7 = bf16[256,512]{1,0:T(8,128)(2,1)S(1)} collective-permute-done((bf16[256,512]{1,0:T(8,128)(2,1)S(1)}, bf16[256,512]{1,0:T(8,128)(2,1)S(1)}, u32[]{:S(2)}, u32[]{:S(2)}) %collective-permute-start.7) | collective-permute-done | bytes 262176 | tf_op jit(solution)/shard_map/ppermute | solution.py:115
  710.9 13.6 %collective-permute-done.11 = bf16[256,512]{1,0:T(8,128)(2,1)S(1)} collective-permute-done((bf16[256,512]{1,0:T(8,128)(2,1)S(1)}, bf16[256,512]{1,0:T(8,128)(2,1)S(1)}, u32[]{:S(2)}, u32[]{:S(2)}) %collective-permute-start.11) | collective-permute-done | bytes 262176 | tf_op jit(solution)/shard_map/ppermute | solution.py:115
  742.6 7.8 fusion.20
  750.4 7.7 fusion.26
  760.4 8.2 fusion.4
  772.6 9.7 %fusion.5 = f32[512,2048]{1,0:T(8,128)} fusion(bf16[2048,2048]{1,0:T(8,128)(2,1)S(1)} %bitcast.317, f32[2048,512]{1,0:T(8,128)} %fusion.18, f32[2048,512]{1,0:T(8,128)} %fusion.14), kind=kOutput, calls=%fused_computation.25 | convolution fusion | flops 4301258752 | bytes 20971520 | tf_op jit(solution)/shard_map/dot_general | solution.py:54
  782.3 6.9 reshape.577
  807.9 18.9 %collective-permute-done.24 = bf16[4,512,256]{2,1,0:T(8,128)(2,1)S(1)} collective-permute-done((bf16[4,512,256]{2,1,0:T(8,128)(2,1)S(1)}, bf16[4,512,256]{2,1,0:T(8,128)(2,1)S(1)}, u32[]{:S(2)}, u32[]{:S(2)}) %collective-permute-start.24) | collective-permute-done | bytes 1048608 | tf_op jit(solution)/shard_map/ppermute | solution.py:115
  834.6 14.9 %collective-permute-done.22 = bf16[256,512]{1,0:T(8,128)(2,1)S(1)} collective-permute-done((bf16[256,512]{1,0:T(8,128)(2,1)S(1)}, bf16[256,512]{1,0:T(8,128)(2,1)S(1)}, u32[]{:S(2)}, u32[]{:S(2)}) %collective-permute-start.22) | collective-permute-done | bytes 262176 | tf_op jit(solution)/shard_map/ppermute | solution.py:115
  849.5 15.1 %collective-permute-done.23 = bf16[256,512]{1,0:T(8,128)(2,1)S(1)} collective-permute-done((bf16[256,512]{1,0:T(8,128)(2,1)S(1)}, bf16[256,512]{1,0:T(8,128)(2,1)S(1)}, u32[]{:S(2)}, u32[]{:S(2)}) %collective-permute-start.23) | collective-permute-done | bytes 262176 | tf_op jit(solution)/shard_map/ppermute | solution.py:115
  869.3 6.6 collective-permute-done.27
  (326 shorter events, 282.1 us)
Async XLA Ops:
  7.9 95.1 %reduce-scatter.5.cloned.1.call-start = ((), (), s32[]{:S(2)}) async-start(), calls=%async_computation.5 | async-start | bytes 2621440 | tf_op jit(solution)/shard_map/reduce_scatter | solution.py:210
  70.2 59.4 %all-gather.11.cloned.1.call-start = ((), (), s32[]{:S(2)}) async-start(), calls=%async_computation.6 | async-start | bytes 2621440 | tf_op jit(solution)/shard_map/all_gather | solution.py:220
  106.4 82.9 %reduce-scatter.7.cloned.1.call-start = ((), (), s32[]{:S(2)}) async-start(), calls=%async_computation.7 | async-start | bytes 2621440 | tf_op jit(solution)/shard_map/reduce_scatter | solution.py:234
  158.1 59.3 %all-gather.13.cloned.1.call-start = ((), (), s32[]{:S(2)}) async-start(), calls=%async_computation.8 | async-start | bytes 2621440 | tf_op jit(solution)/shard_map/all_gather | solution.py:246
  194.2 87.4 %reduce-scatter.9.cloned.1.call-start = ((), (), s32[]{:S(2)}) async-start(), calls=%async_computation.9 | async-start | bytes 2621440 | tf_op jit(solution)/shard_map/reduce_scatter | solution.py:273
  250.5 77.5 %all-gather.17.cloned.1.call-start = ((), (), s32[]{:S(2)}) async-start(), calls=%async_computation.12 | async-start | bytes 2621440 | tf_op jit(solution)/shard_map/all_gather | solution.py:226
  251.2 102.6 %all-gather.15.cloned.1.call-start = ((), (), s32[]{:S(2)}) async-start(), calls=%async_computation.10 | async-start | bytes 2621440 | tf_op jit(solution)/shard_map/all_gather | solution.py:280
  286.1 113.6 %all-gather.21.cloned.1.call-start = ((), (), s32[]{:S(2)}) async-start(), calls=%async_computation.14 | async-start | bytes 2621440 | tf_op jit(solution)/shard_map/all_gather | solution.py:226
  286.9 173.7 %all-gather.19.cloned.1.call-start = ((), (), s32[]{:S(2)}) async-start(), calls=%async_computation.13 | async-start | bytes 10485760 | tf_op jit(solution)/shard_map/all_gather | solution.py:227
  328.0 412.5 %reduce-scatter.11.cloned.1.call-start = ((), (), s32[]{:S(2)}) async-start(), calls=%async_computation.11 | async-start | bytes 2621440 | tf_op jit(solution)/shard_map/reduce_scatter | solution.py:307
  395.6 347.0 %all-gather.23.cloned.1.call-start = ((), (), s32[]{:S(2)}) async-start(), calls=%async_computation.15 | async-start | bytes 10485760 | tf_op jit(solution)/shard_map/all_gather | solution.py:227
  500.9 147.4 %collective-permute-start = (bf16[4,256,512]{2,1,0:T(8,128)(2,1)}, bf16[4,256,512]{2,1,0:T(8,128)(2,1)}, u32[]{:S(2)}, u32[]{:S(2)}) collective-permute-start(bf16[4,256,512]{2,1,0:T(8,128)(2,1)} %bitcast.298), channel_id=1, source_target_pairs={{0,4},{4,0},{8,12},{12,8},{16,20},{20,16},{24,28},{28,24},{1,5},{5... | collective-permute-start | bytes 3145736 | tf_op jit(solution)/shard_map/ppermute | solution.py:115
  523.5 130.4 %collective-permute-start.4 = (bf16[4,256,512]{2,1,0:T(8,128)(2,1)}, bf16[4,256,512]{2,1,0:T(8,128)(2,1)}, u32[]{:S(2)}, u32[]{:S(2)}) collective-permute-start(bf16[4,256,512]{2,1,0:T(8,128)(2,1)} %bitcast.297), channel_id=1, source_target_pairs={{0,4},{4,0},{8,12},{12,8},{16,20},{20,16},{24,28},{28,24},{1,5},{5... | collective-permute-start | bytes 3145736 | tf_op jit(solution)/shard_map/ppermute | solution.py:115
  542.2 113.6 %collective-permute-start.8 = (bf16[4,256,512]{2,1,0:T(8,128)(2,1)}, bf16[4,256,512]{2,1,0:T(8,128)(2,1)}, u32[]{:S(2)}, u32[]{:S(2)}) collective-permute-start(bf16[4,256,512]{2,1,0:T(8,128)(2,1)} %bitcast.296), channel_id=1, source_target_pairs={{0,4},{4,0},{8,12},{12,8},{16,20},{20,16},{24,28},{28,24},{1,5},{5... | collective-permute-start | bytes 3145736 | tf_op jit(solution)/shard_map/ppermute | solution.py:115
  548.5 109.2 %collective-permute-start.12 = (bf16[4,512,256]{2,1,0:T(8,128)(2,1)}, bf16[4,512,256]{2,1,0:T(8,128)(2,1)}, u32[]{:S(2)}, u32[]{:S(2)}) collective-permute-start(bf16[4,512,256]{2,1,0:T(8,128)(2,1)} %fusion.56), channel_id=1, source_target_pairs={{0,4},{4,0},{8,12},{12,8},{16,20},{20,16},{24,28},{28,24},{1,5},{5... | collective-permute-start | bytes 3145736 | tf_op jit(solution)/shard_map/ppermute | solution.py:115
  651.0 31.7 %collective-permute-start.2 = (bf16[256,512]{1,0:T(8,128)(2,1)S(1)}, bf16[256,512]{1,0:T(8,128)(2,1)S(1)}, u32[]{:S(2)}, u32[]{:S(2)}) collective-permute-start(bf16[256,512]{1,0:T(8,128)(2,1)S(1)} %get-tuple-element.70), channel_id=1, source_target_pairs={{0,16},{4,20},{8,24},{12,28},{16,0},{20,4},{24,8},{28,12},{1,17},{... | collective-permute-start | bytes 786440 | tf_op jit(solution)/shard_map/ppermute | solution.py:115
  655.7 46.2 %collective-permute-start.7 = (bf16[256,512]{1,0:T(8,128)(2,1)S(1)}, bf16[256,512]{1,0:T(8,128)(2,1)S(1)}, u32[]{:S(2)}, u32[]{:S(2)}) collective-permute-start(bf16[256,512]{1,0:T(8,128)(2,1)S(1)} %get-tuple-element.66), channel_id=1, source_target_pairs={{0,24},{4,28},{8,16},{12,20},{16,8},{20,12},{24,0},{28,4},{1,25},{... | collective-permute-start | bytes 786440 | tf_op jit(solution)/shard_map/ppermute | solution.py:115
  657.8 48.1 %collective-permute-start.6 = (bf16[256,512]{1,0:T(8,128)(2,1)S(1)}, bf16[256,512]{1,0:T(8,128)(2,1)S(1)}, u32[]{:S(2)}, u32[]{:S(2)}) collective-permute-start(bf16[256,512]{1,0:T(8,128)(2,1)S(1)} %get-tuple-element.67), channel_id=1, source_target_pairs={{0,16},{4,20},{8,24},{12,28},{16,0},{20,4},{24,8},{28,12},{1,17},{... | collective-permute-start | bytes 786440 | tf_op jit(solution)/shard_map/ppermute | solution.py:115
  668.2 38.7 %collective-permute-start.5 = (bf16[256,512]{1,0:T(8,128)(2,1)S(1)}, bf16[256,512]{1,0:T(8,128)(2,1)S(1)}, u32[]{:S(2)}, u32[]{:S(2)}) collective-permute-start(bf16[256,512]{1,0:T(8,128)(2,1)S(1)} %get-tuple-element.65), channel_id=1, source_target_pairs={{0,8},{4,12},{8,0},{12,4},{16,24},{20,28},{24,16},{28,20},{1,9},{5... | collective-permute-start | bytes 786440 | tf_op jit(solution)/shard_map/ppermute | solution.py:115
  682.7 41.8 %collective-permute-start.11 = (bf16[256,512]{1,0:T(8,128)(2,1)S(1)}, bf16[256,512]{1,0:T(8,128)(2,1)S(1)}, u32[]{:S(2)}, u32[]{:S(2)}) collective-permute-start(bf16[256,512]{1,0:T(8,128)(2,1)S(1)} %get-tuple-element.63), channel_id=1, source_target_pairs={{0,24},{4,28},{8,16},{12,20},{16,8},{20,12},{24,0},{28,4},{1,25},{... | collective-permute-start | bytes 786440 | tf_op jit(solution)/shard_map/ppermute | solution.py:115
  683.8 44.5 %collective-permute-start.10 = (bf16[256,512]{1,0:T(8,128)(2,1)S(1)}, bf16[256,512]{1,0:T(8,128)(2,1)S(1)}, u32[]{:S(2)}, u32[]{:S(2)}) collective-permute-start(bf16[256,512]{1,0:T(8,128)(2,1)S(1)} %get-tuple-element.64), channel_id=1, source_target_pairs={{0,16},{4,20},{8,24},{12,28},{16,0},{20,4},{24,8},{28,12},{1,17},{... | collective-permute-start | bytes 786440 | tf_op jit(solution)/shard_map/ppermute | solution.py:115
  706.9 32.7 %collective-permute-start.14 = (bf16[512,256]{1,0:T(8,128)(2,1)S(1)}, bf16[512,256]{1,0:T(8,128)(2,1)S(1)}, u32[]{:S(2)}, u32[]{:S(2)}) collective-permute-start(bf16[512,256]{1,0:T(8,128)(2,1)S(1)} %get-tuple-element.61), channel_id=1, source_target_pairs={{0,16},{4,20},{8,24},{12,28},{16,0},{20,4},{24,8},{28,12},{1,17},{... | collective-permute-start | bytes 786440 | tf_op jit(solution)/shard_map/ppermute | solution.py:115
  759.2 37.0 %collective-permute-start.16 = (bf16[4,256,512]{2,1,0:T(8,128)(2,1)}, bf16[4,256,512]{2,1,0:T(8,128)(2,1)}, u32[]{:S(2)}, u32[]{:S(2)}) collective-permute-start(bf16[4,256,512]{2,1,0:T(8,128)(2,1)} %fusion.58), channel_id=1, source_target_pairs={{0,4},{4,0},{8,12},{12,8},{16,20},{20,16},{24,28},{28,24},{1,5},{5... | collective-permute-start | bytes 3145736 | tf_op jit(solution)/shard_map/ppermute | solution.py:115
  771.7 32.5 %collective-permute-start.20 = (bf16[4,256,512]{2,1,0:T(8,128)(2,1)}, bf16[4,256,512]{2,1,0:T(8,128)(2,1)S(1)}, u32[]{:S(2)}, u32[]{:S(2)}) collective-permute-start(bf16[4,256,512]{2,1,0:T(8,128)(2,1)} %fusion.59), channel_id=1, source_target_pairs={{0,4},{4,0},{8,12},{12,8},{16,20},{20,16},{24,28},{28,24},{1,5},{5... | collective-permute-start | bytes 3145736 | tf_op jit(solution)/shard_map/ppermute | solution.py:115
  793.8 32.9 %collective-permute-start.24 = (bf16[4,512,256]{2,1,0:T(8,128)(2,1)S(1)}, bf16[4,512,256]{2,1,0:T(8,128)(2,1)S(1)}, u32[]{:S(2)}, u32[]{:S(2)}) collective-permute-start(bf16[4,512,256]{2,1,0:T(8,128)(2,1)S(1)} %bitcast.299), channel_id=1, source_target_pairs={{0,4},{4,0},{8,12},{12,8},{16,20},{20,16},{24,28},{28,24},{1,5},{5... | collective-permute-start | bytes 3145736 | tf_op jit(solution)/shard_map/ppermute | solution.py:115
  798.2 32.3 %collective-permute-start.17 = (bf16[256,512]{1,0:T(8,128)(2,1)S(1)}, bf16[256,512]{1,0:T(8,128)(2,1)S(1)}, u32[]{:S(2)}, u32[]{:S(2)}) collective-permute-start(bf16[256,512]{1,0:T(8,128)(2,1)S(1)} %get-tuple-element.57), channel_id=1, source_target_pairs={{0,8},{4,12},{8,0},{12,4},{16,24},{20,28},{24,16},{28,20},{1,9},{5... | collective-permute-start | bytes 786440 | tf_op jit(solution)/shard_map/ppermute | solution.py:115
  801.3 30.4 %collective-permute-start.18 = (bf16[256,512]{1,0:T(8,128)(2,1)S(1)}, bf16[256,512]{1,0:T(8,128)(2,1)S(1)}, u32[]{:S(2)}, u32[]{:S(2)}) collective-permute-start(bf16[256,512]{1,0:T(8,128)(2,1)S(1)} %get-tuple-element.56), channel_id=1, source_target_pairs={{0,16},{4,20},{8,24},{12,28},{16,0},{20,4},{24,8},{28,12},{1,17},{... | collective-permute-start | bytes 786440 | tf_op jit(solution)/shard_map/ppermute | solution.py:115
  801.4 30.4 %collective-permute-start.19 = (bf16[256,512]{1,0:T(8,128)(2,1)S(1)}, bf16[256,512]{1,0:T(8,128)(2,1)S(1)}, u32[]{:S(2)}, u32[]{:S(2)}) collective-permute-start(bf16[256,512]{1,0:T(8,128)(2,1)S(1)} %get-tuple-element.55), channel_id=1, source_target_pairs={{0,24},{4,28},{8,16},{12,20},{16,8},{20,12},{24,0},{28,4},{1,25},{... | collective-permute-start | bytes 786440 | tf_op jit(solution)/shard_map/ppermute | solution.py:115
  830.5 34.2 %collective-permute-start.23 = (bf16[256,512]{1,0:T(8,128)(2,1)S(1)}, bf16[256,512]{1,0:T(8,128)(2,1)S(1)}, u32[]{:S(2)}, u32[]{:S(2)}) collective-permute-start(bf16[256,512]{1,0:T(8,128)(2,1)S(1)} %get-tuple-element.47), channel_id=1, source_target_pairs={{0,24},{4,28},{8,16},{12,20},{16,8},{20,12},{24,0},{28,4},{1,25},{... | collective-permute-start | bytes 786440 | tf_op jit(solution)/shard_map/ppermute | solution.py:115
  831.7 33.0 %collective-permute-start.25 = (bf16[512,256]{1,0:T(8,128)(2,1)S(1)}, bf16[512,256]{1,0:T(8,128)(2,1)S(1)}, u32[]{:S(2)}, u32[]{:S(2)}) collective-permute-start(bf16[512,256]{1,0:T(8,128)(2,1)S(1)} %get-tuple-element.41), channel_id=1, source_target_pairs={{0,8},{4,12},{8,0},{12,4},{16,24},{20,28},{24,16},{28,20},{1,9},{5... | collective-permute-start | bytes 786440 | tf_op jit(solution)/shard_map/ppermute | solution.py:115
  831.9 37.3 %collective-permute-start.26 = (bf16[512,256]{1,0:T(8,128)(2,1)S(1)}, bf16[512,256]{1,0:T(8,128)(2,1)S(1)}, u32[]{:S(2)}, u32[]{:S(2)}) collective-permute-start(bf16[512,256]{1,0:T(8,128)(2,1)S(1)} %get-tuple-element.40), channel_id=1, source_target_pairs={{0,16},{4,20},{8,24},{12,28},{16,0},{20,4},{24,8},{28,12},{1,17},{... | collective-permute-start | bytes 786440 | tf_op jit(solution)/shard_map/ppermute | solution.py:115
  833.4 42.5 %collective-permute-start.27 = (bf16[512,256]{1,0:T(8,128)(2,1)S(1)}, bf16[512,256]{1,0:T(8,128)(2,1)S(1)}, u32[]{:S(2)}, u32[]{:S(2)}) collective-permute-start(bf16[512,256]{1,0:T(8,128)(2,1)S(1)} %get-tuple-element.39), channel_id=1, source_target_pairs={{0,24},{4,28},{8,16},{12,20},{16,8},{20,12},{24,0},{28,4},{1,25},{... | collective-permute-start | bytes 786440 | tf_op jit(solution)/shard_map/ppermute | solution.py:115
  (69 other events, 836.6 us)
Sparse Core Ops, SparseCore 0:
  9.6 24.1 all-gather.8
  70.3 32.6 reduce-scatter.4
  106.5 23.0 all-gather.10
  158.2 31.0 reduce-scatter.6
  194.4 22.9 all-gather.12
  250.6 31.0 reduce-scatter.8
  283.9 44.0 all-gather.16
  330.2 23.5 all-gather.14
  356.0 43.6 all-gather.20
  401.2 59.2 all-gather.18
  463.8 30.9 reduce-scatter.10
  496.2 58.7 all-gather.22
where the time goes:
time: 898 us; the launch traced here: 888 us
  waiting for transfers between devices  420 us (47%)
  matrix products  149 us (17%)
  local copies, waits for them, and re-layouts  124 us (14%)
  blocking collectives  82.2 us (9%)
  other arithmetic  56.8 us (6%)
  starting transfers between devices  38.8 us (4%)
  between operations  15.9 us (2%)
    ppermute x28, waiting for transfers between devices, swap(): return lax.ppermute(value, 'dp', [(d, d ^ shift) for d in range(size)])  125 us
    psum x1, blocking collectives, body(): gain_total = lax.psum(gain_stack, ('dp', 'tensor'))  71.2 us
    all_gather x2, waiting for transfers between devices, gather_group(): return lax.all_gather(part, 'tensor', axis=0, tiled=True)  60.7 us
    dot_general x8, matrix products, times_t(): lax.dot_general(left_mat, right_mat, (((1,), (1,)), ((), ())), preferred_...  49.7 us
    all_gather x2, waiting for transfers between devices, gather_group(): lax.all_gather(shard, 'dp', axis=0, tiled=True, axis_index_groups=groups)  45.1 us
    another operation x12, local copies, waits for them, and re-layouts  42.2 us
    ppermute x28, starting transfers between devices, swap(): return lax.ppermute(value, 'dp', [(d, d ^ shift) for d in range(size)])  37.8 us
    dot_general x7, matrix products, t_times(): lax.dot_general(left_mat, right_mat, (((0,), (0,)), ((), ())), preferred_...  36.6 us
  transfers between devices with their start and end apart: 40, of which 24 were waited for; matrix products, arithmetic and copies ran while one was open for 23% of the time, Pallas kernels for 0%

commit v1 on v0

--- a/solution.py
+++ b/solution.py
@@ -320,7 +320,8 @@
     q_full = lax.dynamic_update_slice(zero_row, grad_gain_query_part, (tensor_start,))
     k_full = lax.dynamic_update_slice(zero_row, grad_gain_key_part, (tensor_start,))
     gain_stack = jnp.stack([q_full, k_full, grad_gain_attn_part, grad_gain_mlp_part])
-    gain_total = lax.psum(gain_stack, ("dp", "tensor"))
+    pieces = lax.all_gather(gain_stack, ("dp", "tensor"), axis=0, tiled=False)
+    gain_total = pieces.sum(axis=0)
     grad_gain_query = lax.dynamic_slice(gain_total[0], (tensor_start,), (local_width,))
     grad_gain_key = lax.dynamic_slice(gain_total[1], (tensor_start,), (local_width,))
     summed = (

time: 898 us -> 835 us (0.930)
  blocking collectives: 82.2 us -> 10.8 us
  waiting for transfers between devices: 420 us -> 431 us
    psum x1 -> x0, blocking collectives: 71.2 us -> none  [body(): gain_total = lax.psum(gain_stack, ('dp', 'tensor'))]
    ppermute x28, waiting for transfers between devices: 125 us -> 138 us  [swap(): return lax.ppermute(value, 'dp', [(d, d ^ shift) for d in range(size)])]
    unnamed x130 -> x126, local copies, waits for them, and re-layouts: 34.7 us -> 35.8 us
  transfers between devices with their start and end apart: 40 -> 41, of which waited for: 24 -> 23; matrix products, arithmetic and copies ran while one was open for 23% -> 25% of each run, Pallas kernels for 0% -> 0%
where the time goes in v1:
time: 835 us; the launch traced here: 822 us
  waiting for transfers between devices  431 us (52%)
  matrix products  153 us (18%)
  local copies, waits for them, and re-layouts  125 us (15%)
  other arithmetic  56.6 us (7%)
  starting transfers between devices  30.4 us (4%)
  between operations  15.6 us (2%)
  blocking collectives  10.8 us (1%)
    ppermute x28, waiting for transfers between devices, swap(): return lax.ppermute(value, 'dp', [(d, d ^ shift) for d in range(size)])  138 us
    all_gather x2, waiting for transfers between devices, gather_group(): return lax.all_gather(part, 'tensor', axis=0, tiled=True)  60.7 us
    dot_general x8, matrix products, times_t(): lax.dot_general(left_mat, right_mat, (((1,), (1,)), ((), ())), preferred_...  49.7 us
    all_gather x2, waiting for transfers between devices, gather_group(): lax.all_gather(shard, 'dp', axis=0, tiled=True, axis_index_groups=groups)  43.1 us
    another operation x12, local copies, waits for them, and re-layouts  41.7 us
    dot_general x7, matrix products, t_times(): lax.dot_general(left_mat, right_mat, (((0,), (0,)), ((), ())), preferred_...  38.6 us
    unnamed x126, local copies, waits for them, and re-layouts  35.8 us
    reduce_scatter x1, waiting for transfers between devices, body(): lax.psum_scatter(jnp.dot(mixed_low, w_out, preferred_element_type=jnp.flo...  32.8 us
  transfers between devices with their start and end apart: 41, of which 23 were waited for; matrix products, arithmetic and copies ran while one was open for 25% of the time, Pallas kernels for 0%

profile of v1, /device:TPU:9, one launch (start us, length us, event | category | flops | bytes accessed | tf_op | source)
XLA Modules:
  0.0 822.3 jit_solution(2138460820404268290)
XLA Ops:
  12.2 21.6 %all-gather.12.cloned.1.call-done = bf16[512,2048]{1,0:T(8,128)(2,1)} async-done(((bf16[128,2048]{1,0:T(8,128)(2,1)}), bf16[512,2048]{1,0:T(8,128)(2,1)}) %all-gather.12.cloned.1.call-update) | async-done | bytes 2097168 | tf_op jit(solution)/shard_map/all_gather | solution.py:186
  70.3 32.8 %reduce-scatter.5.cloned.1.call-done = bf16[128,2048]{1,0:T(8,128)(2,1)} async-done(((bf16[512,2048]{1,0:T(8,128)(2,1)}), bf16[128,2048]{1,0:T(8,128)(2,1)}) %reduce-scatter.5.cloned.1.call-update) | async-done | bytes 524304 | tf_op jit(solution)/shard_map/reduce_scatter | solution.py:210
  106.9 22.8 %all-gather.14.cloned.1.call-done = bf16[512,2048]{1,0:T(8,128)(2,1)} async-done(((bf16[128,2048]{1,0:T(8,128)(2,1)}), bf16[512,2048]{1,0:T(8,128)(2,1)}) %all-gather.14.cloned.1.call-update) | async-done | bytes 2097168 | tf_op jit(solution)/shard_map/all_gather | solution.py:220
  129.6 8.6 %fusion.92 = f32[512,2048]{1,0:T(8,128)S(1)} fusion(bf16[512,2048]{1,0:T(8,128)(2,1)} %all-gather.14.cloned.1.call-done, bf16[2048,2048]{1,0:T(8,128)(2,1)} %param.20), kind=kOutput, calls=%fused_computation.245 | convolution fusion | flops 4294967296 | bytes 14680064 | tf_op jit(solution)/shard_map/dot_general | solution.py:230
  138.2 8.4 %fusion.93 = f32[512,2048]{1,0:T(8,128)S(1)} fusion(bf16[512,2048]{1,0:T(8,128)(2,1)S(1)} %copy-done.50, bf16[2048,2048]{1,0:T(8,128)(2,1)} %param.21), kind=kOutput, calls=%fused_computation.246 | convolution fusion | flops 4294967296 | bytes 14680064 | tf_op jit(solution)/shard_map/dot_general | solution.py:231
  148.7 9.5 %convolution_convert_fusion = bf16[512,2048]{1,0:T(8,128)(2,1)} fusion(bf16[2048,2048]{1,0:T(8,128)(2,1)} %param.22, f32[512,2048]{1,0:T(8,128)S(1)} %fusion.93, f32[512,2048]{1,0:T(8,128)S(1)} %fusion.92), kind=kOutput, calls=%fused_computation.21 | convolution fusion | flops 4302307328 | bytes 18874368 | tf_op jit(solution)/shard_map/dot_general | solution.py:235
  158.2 31.1 %reduce-scatter.7.cloned.1.call-done = bf16[128,2048]{1,0:T(8,128)(2,1)} async-done(((bf16[512,2048]{1,0:T(8,128)(2,1)}), bf16[128,2048]{1,0:T(8,128)(2,1)}) %reduce-scatter.7.cloned.1.call-update) | async-done | bytes 524304 | tf_op jit(solution)/shard_map/reduce_scatter | solution.py:234
  194.3 23.1 %all-gather.16.cloned.1.call-done = bf16[512,2048]{1,0:T(8,128)(2,1)} async-done(((bf16[128,2048]{1,0:T(8,128)(2,1)}), bf16[512,2048]{1,0:T(8,128)(2,1)}) %all-gather.16.cloned.1.call-update) | async-done | bytes 2097168 | tf_op jit(solution)/shard_map/all_gather | solution.py:246
  217.5 7.6 fusion.94
  225.1 13.6 %fusion.25 = f32[512,2048]{1,0:T(8,128)} fusion(bf16[2048,2048]{1,0:T(8,128)(2,1)} %param.20, f32[512,2048]{1,0:T(8,128)} %copy-done.51, f32[512,2048]{1,0:T(8,128)S(1)} %fusion.94, f32[512,2048]{1,0:T(8,128)} %copy-done.52), kind=kOutput, calls=%fused_computation.56 | convolution fusion | flops 4305453056 | bytes 25165824 | tf_op jit(solution)/shard_map/dot_general | solution.py:48
  238.7 11.8 %add_convert_fusion.1 = bf16[512,2048]{1,0:T(8,128)(2,1)} fusion(f32[512,2048]{1,0:T(8,128)} %fusion.25, bf16[2048,2048]{1,0:T(8,128)(2,1)} %param.21, f32[512,2048]{1,0:T(8,128)S(1)} %fusion.94, f32[512,2048]{1,0:T(8,128)} %copy-done.51), kind=kOutput, calls=%fused_computation.8 | convolution fusion | flops 4303355904 | bytes 23068672 | tf_op jit(solution)/shard_map/dot_general | solution.py:48
  251.3 30.4 %reduce-scatter.9.cloned.1.call-done = bf16[128,2048]{1,0:T(8,128)(2,1)} async-done(((bf16[512,2048]{1,0:T(8,128)(2,1)}), bf16[128,2048]{1,0:T(8,128)(2,1)}) %reduce-scatter.9.cloned.1.call-update) | async-done | bytes 524304 | tf_op jit(solution)/shard_map/reduce_scatter | solution.py:273
  287.0 41.1 %all-gather.20.cloned.1.call-done = bf16[512,2048]{1,0:T(8,128)(2,1)} async-done(((bf16[128,2048]{1,0:T(8,128)(2,1)}), bf16[512,2048]{1,0:T(8,128)(2,1)}) %all-gather.20.cloned.1.call-update) | async-done | bytes 2097168 | tf_op jit(solution)/shard_map/all_gather | solution.py:226
  328.3 25.5 %all-gather.18.cloned.1.call-done = bf16[512,2048]{1,0:T(8,128)(2,1)} async-done(((bf16[128,2048]{1,0:T(8,128)(2,1)}), bf16[512,2048]{1,0:T(8,128)(2,1)}) %all-gather.18.cloned.1.call-update) | async-done | bytes 2097168 | tf_op jit(solution)/shard_map/all_gather | solution.py:280
  399.9 60.7 %all-gather.22.cloned.1.call-done = bf16[2048,2048]{1,0:T(8,128)(2,1)} async-done(((bf16[512,2048]{1,0:T(8,128)(2,1)}), bf16[2048,2048]{1,0:T(8,128)(2,1)}) %all-gather.22.cloned.1.call-update) | async-done | bytes 8388624 | tf_op jit(solution)/shard_map/all_gather | solution.py:227
  460.6 10.6 %fusion.14 = f32[2048,512]{1,0:T(8,128)} fusion(bf16[2048,2048]{1,0:T(8,128)(2,1)} %all-gather.22.cloned.1.call-done, bf16[2048,2048]{1,0:T(8,128)(2,1)} %param.20, s32[]{:T(128)S(6)} %select_n.141), kind=kOutput, calls=%fused_computation.44 | convolution fusion | flops 4294967296 | bytes 14680068 | tf_op jit(solution)/shard_map/dot_general | solution.py:257
  471.3 8.3 %fusion.18 = f32[2048,512]{1,0:T(8,128)} fusion(bf16[2048,2048]{1,0:T(8,128)(2,1)S(1)} %copy-done.48, bf16[2048,2048]{1,0:T(8,128)(2,1)} %param.21, s32[]{:T(128)S(6)} %select_n.141), kind=kOutput, calls=%fused_computation.48 | convolution fusion | flops 4294967296 | bytes 14680068 | tf_op jit(solution)/shard_map/dot_general | solution.py:258
  482.8 6.6 reshape.572
  526.7 6.8 reshape.574
  584.1 8.7 %collective-permute-done.8 = bf16[4,256,512]{2,1,0:T(8,128)(2,1)} collective-permute-done((bf16[4,256,512]{2,1,0:T(8,128)(2,1)}, bf16[4,256,512]{2,1,0:T(8,128)(2,1)}, u32[]{:S(2)}, u32[]{:S(2)}) %collective-permute-start.8) | collective-permute-done | bytes 1048608 | tf_op jit(solution)/shard_map/ppermute | solution.py:115
  595.7 19.5 %collective-permute-done.12 = bf16[4,512,256]{2,1,0:T(8,128)(2,1)S(1)} collective-permute-done((bf16[4,512,256]{2,1,0:T(8,128)(2,1)S(1)}, bf16[4,512,256]{2,1,0:T(8,128)(2,1)S(1)}, u32[]{:S(2)}, u32[]{:S(2)}) %collective-permute-start.12) | collective-permute-done | bytes 1048608 | tf_op jit(solution)/shard_map/ppermute | solution.py:115
  622.5 8.0 collective-permute-done.6
  634.0 13.2 %collective-permute-done.11 = bf16[256,512]{1,0:T(8,128)(2,1)S(1)} collective-permute-done((bf16[256,512]{1,0:T(8,128)(2,1)S(1)}, bf16[256,512]{1,0:T(8,128)(2,1)S(1)}, u32[]{:S(2)}, u32[]{:S(2)}) %collective-permute-start.11) | collective-permute-done | bytes 262176 | tf_op jit(solution)/shard_map/ppermute | solution.py:115
  648.2 14.6 %collective-permute-done.10 = bf16[256,512]{1,0:T(8,128)(2,1)S(1)} collective-permute-done((bf16[256,512]{1,0:T(8,128)(2,1)S(1)}, bf16[256,512]{1,0:T(8,128)(2,1)S(1)}, u32[]{:S(2)}, u32[]{:S(2)}) %collective-permute-start.10) | collective-permute-done | bytes 262176 | tf_op jit(solution)/shard_map/ppermute | solution.py:115
  680.2 7.8 fusion.20
  688.0 7.7 fusion.26
  697.6 8.4 %fusion.4 = f32[2048,512]{1,0:T(8,128)S(1)} fusion(bf16[2048,2048]{1,0:T(8,128)(2,1)S(1)} %bitcast.317, f32[2048,512]{1,0:T(8,128)S(1)} %fusion.20, f32[2048,512]{1,0:T(8,128)} %fusion.14), kind=kOutput, calls=%fused_computation.24 | convolution fusion | flops 4301258752 | bytes 20971520 | tf_op jit(solution)/shard_map/dot_general | solution.py:54
  710.0 9.8 %fusion.5 = f32[512,2048]{1,0:T(8,128)} fusion(bf16[2048,2048]{1,0:T(8,128)(2,1)S(1)} %bitcast.319, f32[2048,512]{1,0:T(8,128)} %fusion.18, f32[2048,512]{1,0:T(8,128)} %fusion.14), kind=kOutput, calls=%fused_computation.25 | convolution fusion | flops 4301258752 | bytes 20971520 | tf_op jit(solution)/shard_map/dot_general | solution.py:54
  719.8 6.9 reshape.577
  744.3 21.8 %collective-permute-done.24 = bf16[4,512,256]{2,1,0:T(8,128)(2,1)S(1)} collective-permute-done((bf16[4,512,256]{2,1,0:T(8,128)(2,1)S(1)}, bf16[4,512,256]{2,1,0:T(8,128)(2,1)S(1)}, u32[]{:S(2)}, u32[]{:S(2)}) %collective-permute-start.24) | collective-permute-done | bytes 1048608 | tf_op jit(solution)/shard_map/ppermute | solution.py:115
  773.0 10.5 %collective-permute-done.22 = bf16[256,512]{1,0:T(8,128)(2,1)S(1)} collective-permute-done((bf16[256,512]{1,0:T(8,128)(2,1)S(1)}, bf16[256,512]{1,0:T(8,128)(2,1)S(1)}, u32[]{:S(2)}, u32[]{:S(2)}) %collective-permute-start.22) | collective-permute-done | bytes 262176 | tf_op jit(solution)/shard_map/ppermute | solution.py:115
  783.6 15.7 %collective-permute-done.23 = bf16[256,512]{1,0:T(8,128)(2,1)S(1)} collective-permute-done((bf16[256,512]{1,0:T(8,128)(2,1)S(1)}, bf16[256,512]{1,0:T(8,128)(2,1)S(1)}, u32[]{:S(2)}, u32[]{:S(2)}) %collective-permute-start.23) | collective-permute-done | bytes 262176 | tf_op jit(solution)/shard_map/ppermute | solution.py:115
  (325 shorter events, 273.2 us)
Async XLA Ops:
  7.9 95.2 %reduce-scatter.5.cloned.1.call-start = ((), (), s32[]{:S(2)}) async-start(), calls=%async_computation.5 | async-start | bytes 2621440 | tf_op jit(solution)/shard_map/reduce_scatter | solution.py:210
  70.2 59.4 %all-gather.14.cloned.1.call-start = ((), (), s32[]{:S(2)}) async-start(), calls=%async_computation.6 | async-start | bytes 2621440 | tf_op jit(solution)/shard_map/all_gather | solution.py:220
  106.5 82.9 %reduce-scatter.7.cloned.1.call-start = ((), (), s32[]{:S(2)}) async-start(), calls=%async_computation.7 | async-start | bytes 2621440 | tf_op jit(solution)/shard_map/reduce_scatter | solution.py:234
  158.2 59.3 %all-gather.16.cloned.1.call-start = ((), (), s32[]{:S(2)}) async-start(), calls=%async_computation.8 | async-start | bytes 2621440 | tf_op jit(solution)/shard_map/all_gather | solution.py:246
  194.3 87.4 %reduce-scatter.9.cloned.1.call-start = ((), (), s32[]{:S(2)}) async-start(), calls=%async_computation.9 | async-start | bytes 2621440 | tf_op jit(solution)/shard_map/reduce_scatter | solution.py:273
  250.5 77.5 %all-gather.20.cloned.1.call-start = ((), (), s32[]{:S(2)}) async-start(), calls=%async_computation.12 | async-start | bytes 2621440 | tf_op jit(solution)/shard_map/all_gather | solution.py:226
  251.3 102.6 %all-gather.18.cloned.1.call-start = ((), (), s32[]{:S(2)}) async-start(), calls=%async_computation.10 | async-start | bytes 2621440 | tf_op jit(solution)/shard_map/all_gather | solution.py:280
  286.2 113.6 %all-gather.24.cloned.1.call-start = ((), (), s32[]{:S(2)}) async-start(), calls=%async_computation.14 | async-start | bytes 2621440 | tf_op jit(solution)/shard_map/all_gather | solution.py:226
  286.9 173.7 %all-gather.22.cloned.1.call-start = ((), (), s32[]{:S(2)}) async-start(), calls=%async_computation.13 | async-start | bytes 10485760 | tf_op jit(solution)/shard_map/all_gather | solution.py:227
  328.1 346.8 %all-gather.28.cloned.1.call-start = ((), (), s32[]{:S(2)}) async-start(), calls=%async_computation.16 | async-start | bytes 1081344 | tf_op jit(solution)/shard_map/all_gather | solution.py:323
  386.2 291.9 %reduce-scatter.11.cloned.1.call-start = ((), (), s32[]{:S(2)}) async-start(), calls=%async_computation.11 | async-start | bytes 2621440 | tf_op jit(solution)/shard_map/reduce_scatter | solution.py:307
  397.7 282.5 %all-gather.26.cloned.1.call-start = ((), (), s32[]{:S(2)}) async-start(), calls=%async_computation.15 | async-start | bytes 10485760 | tf_op jit(solution)/shard_map/all_gather | solution.py:227
  500.7 76.6 %collective-permute-start = (bf16[4,256,512]{2,1,0:T(8,128)(2,1)}, bf16[4,256,512]{2,1,0:T(8,128)(2,1)}, u32[]{:S(2)}, u32[]{:S(2)}) collective-permute-start(bf16[4,256,512]{2,1,0:T(8,128)(2,1)} %bitcast.300), channel_id=1, source_target_pairs={{0,4},{4,0},{8,12},{12,8},{16,20},{20,16},{24,28},{28,24},{1,5},{5... | collective-permute-start | bytes 3145736 | tf_op jit(solution)/shard_map/ppermute | solution.py:115
  523.1 58.4 %collective-permute-start.4 = (bf16[4,256,512]{2,1,0:T(8,128)(2,1)}, bf16[4,256,512]{2,1,0:T(8,128)(2,1)}, u32[]{:S(2)}, u32[]{:S(2)}) collective-permute-start(bf16[4,256,512]{2,1,0:T(8,128)(2,1)} %bitcast.298), channel_id=1, source_target_pairs={{0,4},{4,0},{8,12},{12,8},{16,20},{20,16},{24,28},{28,24},{1,5},{5... | collective-permute-start | bytes 3145736 | tf_op jit(solution)/shard_map/ppermute | solution.py:115
  576.8 38.4 %collective-permute-start.12 = (bf16[4,512,256]{2,1,0:T(8,128)(2,1)S(1)}, bf16[4,512,256]{2,1,0:T(8,128)(2,1)S(1)}, u32[]{:S(2)}, u32[]{:S(2)}) collective-permute-start(bf16[4,512,256]{2,1,0:T(8,128)(2,1)S(1)} %fusion.56), channel_id=1, source_target_pairs={{0,4},{4,0},{8,12},{12,8},{16,20},{20,16},{24,28},{28,24},{1,5},{5... | collective-permute-start | bytes 3145736 | tf_op jit(solution)/shard_map/ppermute | solution.py:115
  579.0 38.7 %collective-permute-start.3 = (bf16[256,512]{1,0:T(8,128)(2,1)S(1)}, bf16[256,512]{1,0:T(8,128)(2,1)S(1)}, u32[]{:S(2)}, u32[]{:S(2)}) collective-permute-start(bf16[256,512]{1,0:T(8,128)(2,1)S(1)} %get-tuple-element.69), channel_id=1, source_target_pairs={{0,24},{4,28},{8,16},{12,20},{16,8},{20,12},{24,0},{28,4},{1,25},{... | collective-permute-start | bytes 786440 | tf_op jit(solution)/shard_map/ppermute | solution.py:115
  580.3 37.8 %collective-permute-start.2 = (bf16[256,512]{1,0:T(8,128)(2,1)S(1)}, bf16[256,512]{1,0:T(8,128)(2,1)S(1)}, u32[]{:S(2)}, u32[]{:S(2)}) collective-permute-start(bf16[256,512]{1,0:T(8,128)(2,1)S(1)} %get-tuple-element.70), channel_id=1, source_target_pairs={{0,16},{4,20},{8,24},{12,28},{16,0},{20,4},{24,8},{28,12},{1,17},{... | collective-permute-start | bytes 786440 | tf_op jit(solution)/shard_map/ppermute | solution.py:115
  581.5 36.9 %collective-permute-start.1 = (bf16[256,512]{1,0:T(8,128)(2,1)S(1)}, bf16[256,512]{1,0:T(8,128)(2,1)S(1)}, u32[]{:S(2)}, u32[]{:S(2)}) collective-permute-start(bf16[256,512]{1,0:T(8,128)(2,1)S(1)} %get-tuple-element.68), channel_id=1, source_target_pairs={{0,8},{4,12},{8,0},{12,4},{16,24},{20,28},{24,16},{28,20},{1,9},{5... | collective-permute-start | bytes 786440 | tf_op jit(solution)/shard_map/ppermute | solution.py:115
  618.4 44.4 %collective-permute-start.10 = (bf16[256,512]{1,0:T(8,128)(2,1)S(1)}, bf16[256,512]{1,0:T(8,128)(2,1)S(1)}, u32[]{:S(2)}, u32[]{:S(2)}) collective-permute-start(bf16[256,512]{1,0:T(8,128)(2,1)S(1)} %get-tuple-element.64), channel_id=1, source_target_pairs={{0,16},{4,20},{8,24},{12,28},{16,0},{20,4},{24,8},{28,12},{1,17},{... | collective-permute-start | bytes 786440 | tf_op jit(solution)/shard_map/ppermute | solution.py:115
  621.5 41.2 %collective-permute-start.9 = (bf16[256,512]{1,0:T(8,128)(2,1)S(1)}, bf16[256,512]{1,0:T(8,128)(2,1)S(1)}, u32[]{:S(2)}, u32[]{:S(2)}) collective-permute-start(bf16[256,512]{1,0:T(8,128)(2,1)S(1)} %get-tuple-element.62), channel_id=1, source_target_pairs={{0,8},{4,12},{8,0},{12,4},{16,24},{20,28},{24,16},{28,20},{1,9},{5... | collective-permute-start | bytes 786440 | tf_op jit(solution)/shard_map/ppermute | solution.py:115
  630.4 37.9 %collective-permute-start.15 = (bf16[512,256]{1,0:T(8,128)(2,1)S(1)}, bf16[512,256]{1,0:T(8,128)(2,1)S(1)}, u32[]{:S(2)}, u32[]{:S(2)}) collective-permute-start(bf16[512,256]{1,0:T(8,128)(2,1)S(1)} %get-tuple-element.60), channel_id=1, source_target_pairs={{0,24},{4,28},{8,16},{12,20},{16,8},{20,12},{24,0},{28,4},{1,25},{... | collective-permute-start | bytes 786440 | tf_op jit(solution)/shard_map/ppermute | solution.py:115
  630.4 43.6 %collective-permute-start.14 = (bf16[512,256]{1,0:T(8,128)(2,1)S(1)}, bf16[512,256]{1,0:T(8,128)(2,1)S(1)}, u32[]{:S(2)}, u32[]{:S(2)}) collective-permute-start(bf16[512,256]{1,0:T(8,128)(2,1)S(1)} %get-tuple-element.61), channel_id=1, source_target_pairs={{0,16},{4,20},{8,24},{12,28},{16,0},{20,4},{24,8},{28,12},{1,17},{... | collective-permute-start | bytes 786440 | tf_op jit(solution)/shard_map/ppermute | solution.py:115
  696.8 37.0 %collective-permute-start.16 = (bf16[4,256,512]{2,1,0:T(8,128)(2,1)}, bf16[4,256,512]{2,1,0:T(8,128)(2,1)}, u32[]{:S(2)}, u32[]{:S(2)}) collective-permute-start(bf16[4,256,512]{2,1,0:T(8,128)(2,1)} %fusion.58), channel_id=1, source_target_pairs={{0,4},{4,0},{8,12},{12,8},{16,20},{20,16},{24,28},{28,24},{1,5},{5... | collective-permute-start | bytes 3145736 | tf_op jit(solution)/shard_map/ppermute | solution.py:115
  709.2 34.5 %collective-permute-start.20 = (bf16[4,256,512]{2,1,0:T(8,128)(2,1)}, bf16[4,256,512]{2,1,0:T(8,128)(2,1)S(1)}, u32[]{:S(2)}, u32[]{:S(2)}) collective-permute-start(bf16[4,256,512]{2,1,0:T(8,128)(2,1)} %fusion.59), channel_id=1, source_target_pairs={{0,4},{4,0},{8,12},{12,8},{16,20},{20,16},{24,28},{28,24},{1,5},{5... | collective-permute-start | bytes 3145736 | tf_op jit(solution)/shard_map/ppermute | solution.py:115
  731.3 34.9 %collective-permute-start.24 = (bf16[4,512,256]{2,1,0:T(8,128)(2,1)S(1)}, bf16[4,512,256]{2,1,0:T(8,128)(2,1)S(1)}, u32[]{:S(2)}, u32[]{:S(2)}) collective-permute-start(bf16[4,512,256]{2,1,0:T(8,128)(2,1)S(1)} %bitcast.299), channel_id=1, source_target_pairs={{0,4},{4,0},{8,12},{12,8},{16,20},{20,16},{24,28},{28,24},{1,5},{5... | collective-permute-start | bytes 3145736 | tf_op jit(solution)/shard_map/ppermute | solution.py:115
  735.8 34.2 %collective-permute-start.17 = (bf16[256,512]{1,0:T(8,128)(2,1)S(1)}, bf16[256,512]{1,0:T(8,128)(2,1)S(1)}, u32[]{:S(2)}, u32[]{:S(2)}) collective-permute-start(bf16[256,512]{1,0:T(8,128)(2,1)S(1)} %get-tuple-element.57), channel_id=1, source_target_pairs={{0,8},{4,12},{8,0},{12,4},{16,24},{20,28},{24,16},{28,20},{1,9},{5... | collective-permute-start | bytes 786440 | tf_op jit(solution)/shard_map/ppermute | solution.py:115
  736.2 33.9 %collective-permute-start.18 = (bf16[256,512]{1,0:T(8,128)(2,1)S(1)}, bf16[256,512]{1,0:T(8,128)(2,1)S(1)}, u32[]{:S(2)}, u32[]{:S(2)}) collective-permute-start(bf16[256,512]{1,0:T(8,128)(2,1)S(1)} %get-tuple-element.56), channel_id=1, source_target_pairs={{0,16},{4,20},{8,24},{12,28},{16,0},{20,4},{24,8},{28,12},{1,17},{... | collective-permute-start | bytes 786440 | tf_op jit(solution)/shard_map/ppermute | solution.py:115
  739.0 32.3 %collective-permute-start.19 = (bf16[256,512]{1,0:T(8,128)(2,1)S(1)}, bf16[256,512]{1,0:T(8,128)(2,1)S(1)}, u32[]{:S(2)}, u32[]{:S(2)}) collective-permute-start(bf16[256,512]{1,0:T(8,128)(2,1)S(1)} %get-tuple-element.55), channel_id=1, source_target_pairs={{0,24},{4,28},{8,16},{12,20},{16,8},{20,12},{24,0},{28,4},{1,25},{... | collective-permute-start | bytes 786440 | tf_op jit(solution)/shard_map/ppermute | solution.py:115
  770.0 29.3 %collective-permute-start.23 = (bf16[256,512]{1,0:T(8,128)(2,1)S(1)}, bf16[256,512]{1,0:T(8,128)(2,1)S(1)}, u32[]{:S(2)}, u32[]{:S(2)}) collective-permute-start(bf16[256,512]{1,0:T(8,128)(2,1)S(1)} %get-tuple-element.47), channel_id=1, source_target_pairs={{0,24},{4,28},{8,16},{12,20},{16,8},{20,12},{24,0},{28,4},{1,25},{... | collective-permute-start | bytes 786440 | tf_op jit(solution)/shard_map/ppermute | solution.py:115
  770.1 29.2 %collective-permute-start.25 = (bf16[512,256]{1,0:T(8,128)(2,1)S(1)}, bf16[512,256]{1,0:T(8,128)(2,1)S(1)}, u32[]{:S(2)}, u32[]{:S(2)}) collective-permute-start(bf16[512,256]{1,0:T(8,128)(2,1)S(1)} %get-tuple-element.41), channel_id=1, source_target_pairs={{0,8},{4,12},{8,0},{12,4},{16,24},{20,28},{24,16},{28,20},{1,9},{5... | collective-permute-start | bytes 786440 | tf_op jit(solution)/shard_map/ppermute | solution.py:115
  771.4 33.5 %collective-permute-start.26 = (bf16[512,256]{1,0:T(8,128)(2,1)S(1)}, bf16[512,256]{1,0:T(8,128)(2,1)S(1)}, u32[]{:S(2)}, u32[]{:S(2)}) collective-permute-start(bf16[512,256]{1,0:T(8,128)(2,1)S(1)} %get-tuple-element.40), channel_id=1, source_target_pairs={{0,16},{4,20},{8,24},{12,28},{16,0},{20,4},{24,8},{28,12},{1,17},{... | collective-permute-start | bytes 786440 | tf_op jit(solution)/shard_map/ppermute | solution.py:115
  772.9 37.6 %collective-permute-start.27 = (bf16[512,256]{1,0:T(8,128)(2,1)S(1)}, bf16[512,256]{1,0:T(8,128)(2,1)S(1)}, u32[]{:S(2)}, u32[]{:S(2)}) collective-permute-start(bf16[512,256]{1,0:T(8,128)(2,1)S(1)} %get-tuple-element.39), channel_id=1, source_target_pairs={{0,24},{4,28},{8,16},{12,20},{16,8},{20,12},{24,0},{28,4},{1,25},{... | collective-permute-start | bytes 786440 | tf_op jit(solution)/shard_map/ppermute | solution.py:115
  (68 other events, 827.5 us)
Sparse Core Ops, SparseCore 0:
  9.6 24.1 all-gather.11
  70.3 32.6 reduce-scatter.4
  106.6 22.9 all-gather.13
  158.3 31.0 reduce-scatter.6
  194.4 22.9 all-gather.15
  250.6 31.0 reduce-scatter.8
  283.9 44.0 all-gather.19
  330.3 23.5 all-gather.17
  356.1 43.6 all-gather.23
  401.3 59.2 all-gather.21
  464.5 53.8 all-gather.27
  521.4 30.9 reduce-scatter.10
  554.0 58.6 all-gather.25
